TPU v7x, 32 devices: a whole 2x2x4 slice. The times are simulated.
32 devices in a mesh: section: 2 (over y), expert: 4 (over z), dp: 4 (over x, core).
Axes of the slice: x: 2, y: 2, z: 4, core: 2. Of those that a mesh axis runs over, the one named last changes fastest.
Arguments:
- residual: bfloat16 [4096, 2048], P(('section', 'expert', 'dp')), may hold values from -12 to 12
- queries: bfloat16 [4096, 1024], P(('section', 'expert', 'dp')), may hold values from -6 to 6
- attn_keys: bfloat16 [4096, 1024], P(('section', 'expert', 'dp')), may hold values from -6 to 6
- attn_values: bfloat16 [4096, 1024], P(('section', 'expert', 'dp')), may hold values from -6 to 6
- out_weight: bfloat16 [1024, 2048], P('expert'), may hold values from -0.1875 to 0.1875
- norm_gain: float32 [2048], replicated, may hold values from 0.25 to 1.75
- gate_weight: bfloat16 [4, 2048, 4096], P('expert', None, 'dp'), may hold values from -0.125 to 0.125
- up_weight: bfloat16 [4, 2048, 4096], P('expert', None, 'dp'), may hold values from -0.125 to 0.125
- down_weight: bfloat16 [4, 4096, 2048], P('expert', 'dp'), may hold values from -0.09375 to 0.09375
- expert_ids: int32 [4096, 1], P(('section', 'expert', 'dp')), may hold values from 0 to 3; in each aligned block of 128 rows (0 to 127, 128 to 255, ...) at most 64 rows name the same one
- out_grad: bfloat16 [4096, 2048], P(('section', 'expert', 'dp')), may hold values from -6 to 6
Outputs:
- layer_out: bfloat16 [4096, 2048], P(('section', 'expert', 'dp'))
- resid_grad: bfloat16 [4096, 2048], P(('section', 'expert', 'dp'))
- query_grad: bfloat16 [4096, 1024], P(('section', 'expert', 'dp'))
- key_grad: bfloat16 [4096, 1024], P(('section', 'expert', 'dp'))
- value_grad: bfloat16 [4096, 1024], P(('section', 'expert', 'dp'))
- weight_grad: float32 [1024, 2048], P('expert')
Inputs may be any that keep to these rules, and one draw needn't show every extreme that they name: `expert_ids`: no expert is named by more than 64 of the 128 rows of one device (an aligned block); in every draw some block names one expert exactly 64 times.
All inputs are finite; a program needn't handle non-finite values.
Results may differ from a plain program's by a relative error of at most 0.023.
Values may be sent and summed in bfloat16 or wider, within the bound.
A program may use at most 128 MiB of HBM per device.

v0:
```python
import math
import jax
import jax.numpy as jnp
from jax import lax
from jax.sharding import PartitionSpec as P

D = 2048
HEADS = 8
HEAD = 128
A = 1024
FF = 4096
epsilon = 1e-06


def contract_last(left_side, right_side):
    return lax.dot_general(
        left_side, right_side, (((1,), (1,)), ((), ())), preferred_element_type=jnp.float32
    )


def contract_first(left_side, right_side):
    return lax.dot_general(
        left_side, right_side, (((0,), (0,)), ((), ())), preferred_element_type=jnp.float32
    )


def shards(
    residual,
    queries,
    attn_keys,
    attn_values,
    out_weight,
    norm_gain,
    gate_weight,
    up_weight,
    down_weight,
    expert_ids,
    out_grad,
):
    tokens_here = residual.shape[0]
    experts = lax.axis_size("expert")
    data_ways = lax.axis_size("dp")
    capacity = max(tokens_here // 8, 2 * tokens_here // experts)
    inv_root = 1.0 / math.sqrt(HEAD)
    keys_all, values_all = (
        lax.all_gather(attn_keys, "dp", axis=0, tiled=True),
        lax.all_gather(attn_values, "dp", axis=0, tiled=True),
    )
    query_heads = queries.reshape(tokens_here, HEADS, HEAD)
    key_heads = keys_all.reshape(-1, HEADS, HEAD)
    value_heads = values_all.reshape(-1, HEADS, HEAD)
    scores = (
        jnp.einsum("thd,shd->hts", query_heads, key_heads, preferred_element_type=jnp.float32)
        * inv_root
    )
    row_peak = jnp.max(scores, axis=-1, keepdims=True)
    exp_scores = jnp.exp(scores - row_peak)
    attn_probs = exp_scores / jnp.sum(exp_scores, axis=-1, keepdims=True)
    probs_low = attn_probs.astype(jnp.bfloat16)
    attended = (
        jnp.einsum("hts,shd->thd", probs_low, value_heads, preferred_element_type=jnp.float32)
        .reshape(tokens_here, A)
        .astype(jnp.bfloat16)
    )
    full_out = lax.all_gather(out_weight, "expert", axis=0, tiled=True)
    hidden = residual.astype(jnp.float32) + jnp.dot(
        attended, full_out, preferred_element_type=jnp.float32
    )
    inv_rms = lax.rsqrt(jnp.mean(hidden * hidden, axis=-1, keepdims=True) + epsilon)
    unit_rows = hidden * inv_rms
    normed = (unit_rows * norm_gain).astype(jnp.bfloat16)
    expert_of = expert_ids[:, 0]
    onehot = (expert_of[:, None] == jnp.arange(experts, dtype=jnp.int32)[None, :]).astype(
        jnp.bfloat16
    )
    row_iota = jnp.arange(tokens_here, dtype=jnp.int32)
    earlier_mask = (row_iota[:, None] > row_iota[None, :]).astype(jnp.bfloat16)
    earlier = jnp.dot(earlier_mask, onehot, preferred_element_type=jnp.float32)
    rank_index = jnp.sum(earlier * onehot.astype(jnp.float32), axis=1).astype(jnp.int32)
    slot_index = expert_of * capacity + rank_index
    empty_rows = jnp.zeros((experts * capacity, D), jnp.bfloat16)
    send_buffer = empty_rows.at[slot_index].set(normed).reshape(experts, capacity, D)
    gate_local = gate_weight[0]
    up_local = up_weight[0]
    down_local = down_weight[0]
    block_width = FF // data_ways
    arrived = lax.all_to_all(send_buffer, "expert", split_axis=0, concat_axis=0, tiled=True)
    piece_rows = arrived.shape[1]
    gathered = lax.all_gather(arrived, "dp", axis=0, tiled=True)
    flattened = gathered.reshape(-1, D)
    gate_pre = jnp.dot(flattened, gate_local, preferred_element_type=jnp.float32)
    up_pre = jnp.dot(flattened, up_local, preferred_element_type=jnp.float32)
    activated = (jax.nn.silu(gate_pre) * up_pre).astype(jnp.bfloat16)
    partial_out = jnp.dot(activated, down_local, preferred_element_type=jnp.float32)
    summed = lax.psum_scatter(
        partial_out.reshape(data_ways * experts, piece_rows, D).astype(jnp.bfloat16),
        "dp",
        scatter_dimension=0,
        tiled=True,
    )
    returned = lax.all_to_all(summed, "expert", split_axis=0, concat_axis=0, tiled=True)
    gate_saved = gate_pre.reshape(data_ways * experts, piece_rows, block_width)
    up_saved = up_pre.reshape(data_ways * experts, piece_rows, block_width)
    expert_back = returned.reshape(experts * capacity, D)[slot_index]
    layer_out = (hidden + expert_back.astype(jnp.float32)).astype(jnp.bfloat16)
    grad_buffer = empty_rows.at[slot_index].set(out_grad).reshape(experts, capacity, D)
    grad_arrived = lax.all_to_all(grad_buffer, "expert", split_axis=0, concat_axis=0, tiled=True)
    grad_gathered = lax.all_gather(grad_arrived, "dp", axis=0, tiled=True)
    grad_flat = grad_gathered.reshape(-1, D)
    gate_pre = gate_saved.reshape(-1, block_width)
    up_pre = up_saved.reshape(-1, block_width)
    sigmoid_gate = jax.nn.sigmoid(gate_pre)
    grad_act = contract_last(grad_flat, down_local)
    grad_gate = (grad_act * up_pre * sigmoid_gate * (1.0 + gate_pre * (1.0 - sigmoid_gate))).astype(
        jnp.bfloat16
    )
    grad_up = (grad_act * jax.nn.silu(gate_pre)).astype(jnp.bfloat16)
    partial_grad = contract_last(grad_gate, gate_local) + contract_last(grad_up, up_local)
    grad_normed_rows = lax.psum_scatter(
        partial_grad.reshape(data_ways * experts, capacity, D).astype(jnp.bfloat16),
        "dp",
        scatter_dimension=0,
        tiled=True,
    )
    grad_returned = lax.all_to_all(
        grad_normed_rows, "expert", split_axis=0, concat_axis=0, tiled=True
    )
    grad_normed = grad_returned.reshape(experts * capacity, D)[slot_index].astype(jnp.float32)
    scaled = grad_normed * norm_gain
    resid_grad = (
        out_grad.astype(jnp.float32)
        + inv_rms * (scaled - unit_rows * jnp.mean(scaled * unit_rows, axis=-1, keepdims=True))
    ).astype(jnp.bfloat16)
    grad_shard = lax.psum_scatter(
        contract_first(attended, resid_grad).astype(jnp.bfloat16),
        "expert",
        scatter_dimension=0,
        tiled=True,
    )
    weight_grad = lax.psum(grad_shard, ("section", "dp")).astype(jnp.float32)
    grad_attended = contract_last(resid_grad, full_out).astype(jnp.bfloat16)
    grad_heads = grad_attended.reshape(tokens_here, HEADS, HEAD)
    grad_probs = jnp.einsum(
        "thd,shd->hts", grad_heads, value_heads, preferred_element_type=jnp.float32
    )
    row_delta = jnp.sum(attn_probs * grad_probs, axis=-1, keepdims=True)
    grad_scores = (attn_probs * (grad_probs - row_delta)).astype(jnp.bfloat16)
    query_grad = (
        (
            jnp.einsum("hts,shd->thd", grad_scores, key_heads, preferred_element_type=jnp.float32)
            * inv_root
        )
        .reshape(tokens_here, A)
        .astype(jnp.bfloat16)
    )
    key_part = (
        jnp.einsum("hts,thd->shd", grad_scores, query_heads, preferred_element_type=jnp.float32)
        * inv_root
    )
    value_part = jnp.einsum(
        "hts,thd->shd", probs_low, grad_heads, preferred_element_type=jnp.float32
    )
    key_value = lax.psum_scatter(
        jnp.concatenate(
            [
                key_part.reshape(lax.axis_size("dp") * tokens_here, A),
                value_part.reshape(lax.axis_size("dp") * tokens_here, A),
            ],
            axis=1,
        ).astype(jnp.bfloat16),
        "dp",
        scatter_dimension=0,
        tiled=True,
    ).astype(jnp.float32)
    key_grad = key_value[:, :A].astype(jnp.bfloat16)
    value_grad = key_value[:, A:].astype(jnp.bfloat16)
    return (layer_out, resid_grad, query_grad, key_grad, value_grad, weight_grad)


def solution(mesh):
    return jax.shard_map(
        shards,
        mesh=mesh,
        in_specs=(
            P(("section", "expert", "dp"), None),
            P(("section", "expert", "dp"), None),
            P(("section", "expert", "dp"), None),
            P(("section", "expert", "dp"), None),
            P("expert", None),
            P(),
            P("expert", None, "dp"),
            P("expert", None, "dp"),
            P("expert", "dp", None),
            P(("section", "expert", "dp"), None),
            P(("section", "expert", "dp"), None),
        ),
        out_specs=(
            P(("section", "expert", "dp"), None),
            P(("section", "expert", "dp"), None),
            P(("section", "expert", "dp"), None),
            P(("section", "expert", "dp"), None),
            P(("section", "expert", "dp"), None),
            P("expert", None),
        ),
        check_vma=False,
    )
```

profile of v0, /device:TPU:0, one launch (start us, length us, event | category | flops | bytes accessed | tf_op | source)
XLA Modules:
  0.0 544.3 jit_solution(3329325886076428349)
XLA Ops:
  7.2 0.7 all-gather.8.cloned.1.call-update
  7.9 1.8 copy.38
  9.8 0.7 all-gather.10.cloned.1.call-update
  10.5 1.1 copy.51
  11.7 0.9 fusion.22
  12.6 0.7 fusion.37
  13.2 15.7 %all-gather.8.cloned.1.call-done = bf16[512,1024]{1,0:T(8,128)(2,1)} async-done(((bf16[128,1024]{1,0:T(8,128)(2,1)}), bf16[512,1024]{1,0:T(8,128)(2,1)}) %all-gather.8.cloned.1.call-update) | async-done | bytes 1048592 | tf_op jit(solution)/shard_map/all_gather | solution.py:47
  29.0 1.5 copy.41
  30.5 17.5 %all-gather.6.cloned.1.call-done = bf16[512,1024]{0,1:T(8,128)(2,1)} async-done(((bf16[128,1024]{0,1:T(8,128)(2,1)}), bf16[512,1024]{0,1:T(8,128)(2,1)}) %all-gather.6.cloned.1.call-update) | async-done | bytes 1048592 | tf_op jit(solution)/shard_map/all_gather | solution.py:46
  48.0 2.1 fusion.42
  50.1 1.4 convolution_convert_fusion.2
  51.5 78.8 %all-gather.10.cloned.1.call-done = bf16[1024,2048]{1,0:T(8,128)(2,1)} async-done(((bf16[256,2048]{1,0:T(8,128)(2,1)}), bf16[1024,2048]{1,0:T(8,128)(2,1)}) %all-gather.10.cloned.1.call-update) | async-done | bytes 4194320 | tf_op jit(solution)/shard_map/all_gather | solution.py:65
  130.3 3.2 multiply_reduce_fusion.3
  133.5 1.8 scatter_custom_fusion
  135.3 29.0 %all_to_all.20 = bf16[4,64,2048]{2,1,0:T(8,128)(2,1)} all-to-all(bf16[4,64,2048]{2,1,0:T(8,128)(2,1)S(1)} %bitcast.80), channel_id=1, replica_groups=mesh['section'=2,'expert'=4,'dp'=4] {'expert'}, dimensions={0} | all-to-all | bytes 2097152 | tf_op jit(solution)/shard_map/all_to_all | solution.py:87
  164.4 2.2 scatter_custom_fusion.1
  166.6 28.4 %all_to_all.21 = bf16[4,64,2048]{2,1,0:T(8,128)(2,1)} all-to-all(bf16[4,64,2048]{2,1,0:T(8,128)(2,1)S(1)} %bitcast.78), channel_id=1, replica_groups=mesh['section'=2,'expert'=4,'dp'=4] {'expert'}, dimensions={0} | all-to-all | bytes 2097152 | tf_op jit(solution)/shard_map/all_to_all | solution.py:107
  195.1 2.9 all-gather.12.cloned.1.call-done
  198.0 7.6 %fusion.11 = f32[1024,1024]{1,0:T(8,128)S(1)} fusion(bf16[1024,2048]{1,0:T(8,128)(2,1)} %bitcast.94, bf16[1,2048,1024]{2,1,0:T(8,128)(2,1)} %param.17), kind=kOutput, calls=%fused_computation.16 | convolution fusion | flops 4294967296 | bytes 12582912 | tf_op jit(solution)/shard_map/dot_general | solution.py:91
  205.7 6.5 %multiply_convert_fusion.2 = (bf16[1024,1024]{1,0:T(8,128)(2,1)S(1)}, f32[1024,1024]{1,0:T(8,128)}) fusion(f32[1024,1024]{1,0:T(8,128)S(1)} %fusion.11, bf16[1024,2048]{1,0:T(8,128)(2,1)S(1)} %bitcast.95, bf16[1,2048,1024]{2,1,0:T(8,128)(2,1)S(1)} %copy-done.10), kind=kOutput, calls=%fused_computation.20 | convolution fusion | flops 4301258752 | bytes 18874368 | tf_op jit(solution)/shard_map/dot_general | solution.py:92
  212.2 6.1 %fusion.14 = bf16[16,64,2048]{2,1,0:T(8,128)(2,1)} fusion(bf16[16,64,1024]{2,1,0:T(8,128)(2,1)S(1)} %bitcast.97, bf16[1,1024,2048]{2,1,0:T(8,128)(2,1)S(1)} %copy-done.9), kind=kOutput, calls=%fused_computation.24 | convolution fusion | flops 4297064448 | bytes 10485760 | tf_op jit(solution)/shard_map/dot_general | solution.py:94
  218.6 15.3 %all-gather.14.cloned.1.call-done = bf16[16,64,2048]{2,1,0:T(8,128)(2,1)} async-done(((bf16[4,64,2048]{2,1,0:T(8,128)(2,1)}), bf16[16,64,2048]{2,1,0:T(8,128)(2,1)}) %all-gather.14.cloned.1.call-update) | async-done | bytes 4194320 | tf_op jit(solution)/shard_map/all_gather | solution.py:108
  233.9 7.7 %fusion.3 = f32[1024,1024]{1,0:T(8,128)S(1)} fusion(bf16[1024,2048]{1,0:T(8,128)(2,1)} %bitcast.93, bf16[1,1024,2048]{2,1,0:T(8,128)(2,1)} %param.19), kind=kOutput, calls=%fused_computation.8 | convolution fusion | flops 4294967296 | bytes 12582912 | tf_op jit(solution)/shard_map/dot_general | solution.py:16
  241.7 6.9 %fusion.5 = f32[1024,2048]{1,0:T(8,128)} fusion(bf16[1,2048,1024]{2,1,0:T(8,128)(2,1)S(1)} %copy-done.11, f32[1024,1024]{1,0:T(8,128)S(1)} %fusion.3, f32[1024,1024]{1,0:T(8,128)S(1)} %copy-done.15), kind=kOutput, calls=%fused_computation.10 | convolution fusion | flops 4301258752 | bytes 20971520 | tf_op jit(solution)/shard_map/dot_general | solution.py:16
  248.5 14.3 %add_convert_fusion = bf16[1024,2048]{1,0:T(8,128)(2,1)} fusion(f32[1024,2048]{1,0:T(8,128)} %fusion.5, bf16[1,2048,1024]{2,1,0:T(8,128)(2,1)S(1)} %copy-done.12, f32[1024,1024]{1,0:T(8,128)} %copy-done.14, f32[1024,1024]{1,0:T(8,128)} %copy-done.16, f32[1024,1024]{1,0:T(8,128)} %get-tuple-element.33), kind=kOutput, calls=%fused_computation.5 | convolution fusion | flops 4309647360 | bytes 29360128 | tf_op jit(solution)/shard_map/dot_general | solution.py:16
  262.9 18.0 %reduce-scatter.5.cloned.1.call-done = bf16[4,64,2048]{2,1,0:T(8,128)(2,1)} async-done(((bf16[16,64,2048]{2,1,0:T(8,128)(2,1)}), bf16[4,64,2048]{2,1,0:T(8,128)(2,1)}) %reduce-scatter.5.cloned.1.call-update) | async-done | bytes 1048592 | tf_op jit(solution)/shard_map/reduce_scatter | solution.py:95
  280.9 4.6 all-to-all-start.1
  285.5 42.6 %reduce-scatter.7.cloned.1.call-done = bf16[4,64,2048]{2,1,0:T(8,128)(2,1)} async-done(((bf16[16,64,2048]{2,1,0:T(8,128)(2,1)}), bf16[4,64,2048]{2,1,0:T(8,128)(2,1)}) %reduce-scatter.7.cloned.1.call-update) | async-done | bytes 1048592 | tf_op jit(solution)/shard_map/reduce_scatter | solution.py:119
  328.1 4.6 all-to-all-start.3
  332.7 1.7 gather_fusion
  334.4 23.8 %all-to-all-done.3 = bf16[4,64,2048]{2,1,0:T(8,128)(2,1)S(1)} async-done(((bf16[4,64,2048]{2,1,0:T(8,128)(2,1)}), bf16[4,64,2048]{2,1,0:T(8,128)(2,1)S(1)}, u32[]{:S(2)}, u32[]{:S(2)}) %all-to-all-start.3) | async-done | bytes 1048608 | tf_op jit(solution)/shard_map/all_to_all | solution.py:125
  358.2 0.9 gather_fusion.1
  359.5 2.4 add_convert_fusion.1
  361.9 3.2 convolution_convert_fusion
  365.3 3.9 convolution_convert_fusion.3
  369.2 0.8 copy.52
  370.1 2.5 convolution_convert_fusion.1
  372.6 2.3 copy.47
  374.9 1.5 multiply_reduce_fusion
  377.2 1.3 copy.46
  378.5 2.8 pad_maximum_fusion
  381.5 58.7 %reduce-scatter.11.cloned.1.call-done = bf16[256,2048]{1,0:T(8,128)(2,1)} async-done(((bf16[1024,2048]{1,0:T(8,128)(2,1)}), bf16[256,2048]{1,0:T(8,128)(2,1)}) %reduce-scatter.11.cloned.1.call-update) | async-done | bytes 1048592 | tf_op jit(solution)/shard_map/reduce_scatter | solution.py:134
  440.2 0.4 fusion.21
  440.6 0.9 copy.48
  441.5 33.5 %reduce-scatter.9.cloned.1.call-done = bf16[128,2048]{1,0:T(8,128)(2,1)} async-done(((bf16[512,2048]{1,0:T(8,128)(2,1)}), bf16[128,2048]{1,0:T(8,128)(2,1)}) %reduce-scatter.9.cloned.1.call-update) | async-done | bytes 524304 | tf_op jit(solution)/shard_map/reduce_scatter | solution.py:163
  475.0 1.9 fusion.41
  476.8 57.9 %all-reduce.2.cloned.1.call-done = bf16[256,2048]{1,0:T(8,128)(2,1)} async-done(((bf16[256,2048]{1,0:T(8,128)(2,1)}), bf16[256,2048]{1,0:T(8,128)(2,1)}) %all-reduce.2.cloned.1.call-update) | async-done | bytes 1048592 | tf_op jit(solution)/shard_map/psum | solution.py:140
  534.7 2.8 convert_element_type.123
  (59 shorter events, 2.1 us)
Async XLA Ops:
  7.2 21.8 %all-gather.8.cloned.1.call-start = ((), (), s32[]{:S(2)}) async-start(), calls=%async_computation.9 | async-start | bytes 1310720 | tf_op jit(solution)/shard_map/all_gather | solution.py:47
  7.9 40.1 %all-gather.6.cloned.1.call-start = ((), (), s32[]{:S(2)}) async-start(), calls=%async_computation.8 | async-start | bytes 1310720 | tf_op jit(solution)/shard_map/all_gather | solution.py:46
  9.8 120.6 %all-gather.10.cloned.1.call-start = ((), (), s32[]{:S(2)}) async-start(), calls=%async_computation.10 | async-start | bytes 5242880 | tf_op jit(solution)/shard_map/all_gather | solution.py:65
  10.5 187.5 %all-gather.12.cloned.1.call-start = ((), (), s32[]{:S(2)}) async-start(), calls=%async_computation.11 | async-start | bytes 5242880 | tf_op jit(solution)/shard_map/all_gather | solution.py:89
  30.5 21.0 %copy-start.6 = (bf16[512,1024]{0,1:T(8,128)(2,1)}, bf16[512,1024]{0,1:T(8,128)(2,1)S(1)}, u32[]{:S(2)}) copy-start(bf16[512,1024]{0,1:T(8,128)(2,1)S(1)} %copy.41) | copy-start | bytes 3145732
  50.1 1.4 copy-start
  51.5 82.0 %copy-start.8 = (f32[2048]{0:T(1024)S(1)}, f32[2048]{0:T(1024)}, u32[]{:S(2)}) copy-start(f32[2048]{0:T(1024)} %param.16) | copy-start | bytes 24580
  164.4 69.5 %all-gather.14.cloned.1.call-start = ((), (), s32[]{:S(2)}) async-start(), calls=%async_computation.13 | async-start | bytes 5242880 | tf_op jit(solution)/shard_map/all_gather | solution.py:108
  195.1 85.8 %reduce-scatter.5.cloned.1.call-start = ((), (), s32[]{:S(2)}) async-start(), calls=%async_computation.12 | async-start | bytes 5242880 | tf_op jit(solution)/shard_map/reduce_scatter | solution.py:95
  198.0 7.7 %copy-start.10 = (bf16[1,2048,1024]{2,1,0:T(8,128)(2,1)S(1)}, bf16[1,2048,1024]{2,1,0:T(8,128)(2,1)}, u32[]{:S(2)}) copy-start(bf16[1,2048,1024]{2,1,0:T(8,128)(2,1)} %param.18) | copy-start | bytes 12582916
  198.0 7.7 %copy-start.13 = (bf16[16,64,2048]{2,1,0:T(8,128)(2,1)S(1)}, bf16[16,64,2048]{2,1,0:T(8,128)(2,1)}, u32[]{:S(2)}) copy-start(bf16[16,64,2048]{2,1,0:T(8,128)(2,1)} %all-gather.12.cloned.1.call-done) | copy-start | bytes 12582916
  205.7 6.6 %copy-start.14 = (f32[1024,1024]{1,0:T(8,128)}, f32[1024,1024]{1,0:T(8,128)S(1)}, u32[]{:S(2)}) copy-start(f32[1024,1024]{1,0:T(8,128)S(1)} %fusion.11) | copy-start | bytes 12582916
  205.7 6.6 %copy-start.9 = (bf16[1,1024,2048]{2,1,0:T(8,128)(2,1)S(1)}, bf16[1,1024,2048]{2,1,0:T(8,128)(2,1)}, u32[]{:S(2)}) copy-start(bf16[1,1024,2048]{2,1,0:T(8,128)(2,1)} %param.19) | copy-start | bytes 12582916
  218.4 109.7 %reduce-scatter.7.cloned.1.call-start = ((), (), s32[]{:S(2)}) async-start(), calls=%async_computation.14 | async-start | bytes 5242880 | tf_op jit(solution)/shard_map/reduce_scatter | solution.py:119
  233.9 7.7 %copy-start.11 = (bf16[1,2048,1024]{2,1,0:T(8,128)(2,1)S(1)}, bf16[1,2048,1024]{2,1,0:T(8,128)(2,1)}, u32[]{:S(2)}) copy-start(bf16[1,2048,1024]{2,1,0:T(8,128)(2,1)} %param.18) | copy-start | bytes 12582916
  233.9 7.7 %copy-start.15 = (f32[1024,1024]{1,0:T(8,128)S(1)}, f32[1024,1024]{1,0:T(8,128)}, u32[]{:S(2)}) copy-start(f32[1024,1024]{1,0:T(8,128)} %copy-done.14) | copy-start | bytes 12582916
  241.7 6.9 %copy-start.16 = (f32[1024,1024]{1,0:T(8,128)}, f32[1024,1024]{1,0:T(8,128)S(1)}, u32[]{:S(2)}) copy-start(f32[1024,1024]{1,0:T(8,128)S(1)} %fusion.3) | copy-start | bytes 12582916
  241.7 6.9 %copy-start.12 = (bf16[1,2048,1024]{2,1,0:T(8,128)(2,1)S(1)}, bf16[1,2048,1024]{2,1,0:T(8,128)(2,1)}, u32[]{:S(2)}) copy-start(bf16[1,2048,1024]{2,1,0:T(8,128)(2,1)} %param.17) | copy-start | bytes 12582916
  280.9 47.2 %all-to-all-start.1 = ((bf16[4,64,2048]{2,1,0:T(8,128)(2,1)}), bf16[4,64,2048]{2,1,0:T(8,128)(2,1)S(1)}, u32[]{:S(2)}, u32[]{:S(2)}) async-start(bf16[4,64,2048]{2,1,0:T(8,128)(2,1)} %reduce-scatter.5.cloned.1.call-done), calls=%async_computation.2 | async-start | bytes 2097152 | tf_op jit(solution)/shard_map/all_to_all | solution.py:101
  328.1 30.1 %all-to-all-start.3 = ((bf16[4,64,2048]{2,1,0:T(8,128)(2,1)}), bf16[4,64,2048]{2,1,0:T(8,128)(2,1)S(1)}, u32[]{:S(2)}, u32[]{:S(2)}) async-start(bf16[4,64,2048]{2,1,0:T(8,128)(2,1)} %reduce-scatter.7.cloned.1.call-done), calls=%async_computation.5 | async-start | bytes 2097152 | tf_op jit(solution)/shard_map/all_to_all | solution.py:125
  332.7 107.5 %reduce-scatter.11.cloned.1.call-start = ((), (), s32[]{:S(2)}) async-start(), calls=%async_computation.16 | async-start | bytes 5242880 | tf_op jit(solution)/shard_map/reduce_scatter | solution.py:134
  359.2 2.7 copy-start.5
  361.9 3.5 copy-start.2
  365.0 5.0 copy-start.1
  365.1 109.9 %reduce-scatter.9.cloned.1.call-start = ((), (), s32[]{:S(2)}) async-start(), calls=%async_computation.15 | async-start | bytes 2621440 | tf_op jit(solution)/shard_map/reduce_scatter | solution.py:163
  370.1 4.8 copy-start.7
  376.8 1.8 copy-start.4
  378.5 61.6 %copy-start.3 = (bf16[512,1024]{0,1:T(8,128)(2,1)S(1)}, bf16[512,1024]{0,1:T(8,128)(2,1)}, u32[]{:S(2)}) copy-start(bf16[512,1024]{0,1:T(8,128)(2,1)} %all-gather.6.cloned.1.call-done) | copy-start | bytes 3145732
  381.4 153.3 %all-reduce.2.cloned.1.call-start = ((), (), s32[]{:S(2)}) async-start(), calls=%async_computation.17 | async-start | bytes 2097152 | tf_op jit(solution)/shard_map/psum | solution.py:140
Sparse Core Ops, SparseCore 0:
  9.5 19.4 all-gather.7
  31.1 16.8 all-gather.5
  49.5 80.7 all-gather.9
  164.5 33.4 all-gather.11
  199.4 34.4 all-gather.13
  236.3 44.5 reduce-scatter.4
  283.4 44.5 reduce-scatter.6
  365.2 74.9 reduce-scatter.10
  443.2 31.6 reduce-scatter.8
  478.0 56.6 all-reduce.1
where the time goes:
time: 545 us; the launch traced here: 544 us
  waiting for transfers between devices  366 us (67%)
  matrix products  68.7 us (13%)
  blocking collectives  57.4 us (11%)
  local copies, waits for them, and re-layouts  16.5 us (3%)
  between operations  14.4 us (3%)
  other arithmetic  11.2 us (2%)
  starting transfers between devices  9.97 us (2%)
    all_gather x1, waiting for transfers between devices, shards(): full_out = lax.all_gather(out_weight, 'expert', axis=0, tiled=True)  78.8 us
    reduce_scatter x1, waiting for transfers between devices, shards(): lax.psum_scatter(contract_first(attended, resid_grad).astype(jnp.bfloat16...  58.7 us
    psum x1, waiting for transfers between devices, shards(): weight_grad = lax.psum(grad_shard, ('section', 'dp')).astype(jnp.float32)  57.9 us
    reduce_scatter x1, waiting for transfers between devices, shards(): lax.psum_scatter(partial_grad.reshape(data_ways * experts, capacity, D).a...  42.6 us
    reduce_scatter x1, waiting for transfers between devices, shards(): lax.psum_scatter(jnp.concatenate([key_part.reshape(lax.axis_size('dp') *...  33.5 us
    dot_general x4, matrix products, contract_last(): lax.dot_general(left_side, right_side, (((1,), (1,)), ((), ())), preferre...  32.7 us
    all_to_all x1, blocking collectives, shards(): lax.all_to_all(send_buffer, 'expert', split_axis=0, concat_axis=0, tiled=...  29 us
    all_to_all x1, blocking collectives, shards(): lax.all_to_all(grad_buffer, 'expert', split_axis=0, concat_axis=0, tiled=...  28.4 us
  transfers between devices with their start and end apart: 12, of which 11 were waited for; matrix products, arithmetic and copies ran while one was open for 15% of the time, Pallas kernels for 0%

commit v1 on v0

--- a/solution.py
+++ b/solution.py
@@ -3,6 +3,7 @@
 import jax.numpy as jnp
 from jax import lax
 from jax.sharding import PartitionSpec as P
+from jax.lax import psum
 
 D = 2048
 HEADS = 8
@@ -137,7 +138,8 @@
         scatter_dimension=0,
         tiled=True,
     )
-    weight_grad = lax.psum(grad_shard, ("section", "dp")).astype(jnp.float32)
+    paths_treat = lambda inp, shard_axis, ax_name: psum(psum(inp, shard_axis), ax_name)
+    weight_grad = paths_treat(grad_shard, "dp", "section").astype(jnp.float32)
     grad_attended = contract_last(resid_grad, full_out).astype(jnp.bfloat16)
     grad_heads = grad_attended.reshape(tokens_here, HEADS, HEAD)
     grad_probs = jnp.einsum(

time: 545 us -> 566 us (1.039)
  waiting for transfers between devices: 366 us -> 388 us
    psum x1 -> x2, waiting for transfers between devices: 57.9 us -> 75.1 us  [the longest x1 40.6 us: shards(): psum(psum(inp, shard_axis), ax_name)]
  transfers between devices with their start and end apart: 12 -> 13, of which waited for: 11 -> 12; matrix products, arithmetic and copies ran while one was open for 15% -> 14% of each run, Pallas kernels for 0% -> 0%
where the time goes in v1:
time: 566 us
  waiting for transfers between devices  388 us (69%)
  matrix products  68.7 us (12%)
  blocking collectives  57.4 us (10%)
  local copies, waits for them, and re-layouts  16.5 us (3%)
  between operations  14.1 us (2%)
  other arithmetic  11.1 us (2%)
  starting transfers between devices  10 us (2%)
    all_gather x1, waiting for transfers between devices, shards(): full_out = lax.all_gather(out_weight, 'expert', axis=0, tiled=True)  78.8 us
    reduce_scatter x1, waiting for transfers between devices, shards(): lax.psum_scatter(contract_first(attended, resid_grad).astype(jnp.bfloat16...  63.3 us
    reduce_scatter x1, waiting for transfers between devices, shards(): lax.psum_scatter(partial_grad.reshape(data_ways * experts, capacity, D).a...  42.6 us
    psum x1, waiting for transfers between devices, shards(): psum(psum(inp, shard_axis), ax_name)  40.6 us
    psum x1, waiting for transfers between devices, shards(): psum(inp, shard_axis)  34.5 us
    reduce_scatter x1, waiting for transfers between devices, shards(): lax.psum_scatter(jnp.concatenate([key_part.reshape(lax.axis_size('dp') *...  33.3 us
    dot_general x4, matrix products, contract_last(): lax.dot_general(left_side, right_side, (((1,), (1,)), ((), ())), preferre...  32.7 us
    all_to_all x1, blocking collectives, shards(): lax.all_to_all(send_buffer, 'expert', split_axis=0, concat_axis=0, tiled=...  29 us
  transfers between devices with their start and end apart: 13, of which 12 were waited for; matrix products, arithmetic and copies ran while one was open for 14% of the time, Pallas kernels for 0%

profile of v1, /device:TPU:0, one launch (start us, length us, event | category | flops | bytes accessed | tf_op | source)
XLA Modules:
  0.0 565.7 jit_solution(1721976271273994731)
XLA Ops:
  7.2 0.7 all-gather.8.cloned.1.call-update
  7.9 1.8 copy.38
  9.8 0.7 all-gather.10.cloned.1.call-update
  10.5 1.1 copy.51
  11.7 0.9 fusion.22
  12.6 0.7 fusion.37
  13.2 15.7 %all-gather.8.cloned.1.call-done = bf16[512,1024]{1,0:T(8,128)(2,1)} async-done(((bf16[128,1024]{1,0:T(8,128)(2,1)}), bf16[512,1024]{1,0:T(8,128)(2,1)}) %all-gather.8.cloned.1.call-update) | async-done | bytes 1048592 | tf_op jit(solution)/shard_map/all_gather | solution.py:48
  29.0 1.5 copy.41
  30.5 17.5 %all-gather.6.cloned.1.call-done = bf16[512,1024]{0,1:T(8,128)(2,1)} async-done(((bf16[128,1024]{0,1:T(8,128)(2,1)}), bf16[512,1024]{0,1:T(8,128)(2,1)}) %all-gather.6.cloned.1.call-update) | async-done | bytes 1048592 | tf_op jit(solution)/shard_map/all_gather | solution.py:47
  48.0 2.1 fusion.42
  50.1 1.4 convolution_convert_fusion.2
  51.5 78.8 %all-gather.10.cloned.1.call-done = bf16[1024,2048]{1,0:T(8,128)(2,1)} async-done(((bf16[256,2048]{1,0:T(8,128)(2,1)}), bf16[1024,2048]{1,0:T(8,128)(2,1)}) %all-gather.10.cloned.1.call-update) | async-done | bytes 4194320 | tf_op jit(solution)/shard_map/all_gather | solution.py:66
  130.3 3.2 multiply_reduce_fusion.3
  133.5 1.8 scatter_custom_fusion
  135.3 29.0 %all_to_all.20 = bf16[4,64,2048]{2,1,0:T(8,128)(2,1)} all-to-all(bf16[4,64,2048]{2,1,0:T(8,128)(2,1)S(1)} %bitcast.80), channel_id=1, replica_groups=mesh['section'=2,'expert'=4,'dp'=4] {'expert'}, dimensions={0} | all-to-all | bytes 2097152 | tf_op jit(solution)/shard_map/all_to_all | solution.py:88
  164.4 2.2 scatter_custom_fusion.1
  166.6 28.4 %all_to_all.21 = bf16[4,64,2048]{2,1,0:T(8,128)(2,1)} all-to-all(bf16[4,64,2048]{2,1,0:T(8,128)(2,1)S(1)} %bitcast.78), channel_id=1, replica_groups=mesh['section'=2,'expert'=4,'dp'=4] {'expert'}, dimensions={0} | all-to-all | bytes 2097152 | tf_op jit(solution)/shard_map/all_to_all | solution.py:108
  195.1 2.9 all-gather.12.cloned.1.call-done
  198.0 7.6 %fusion.11 = f32[1024,1024]{1,0:T(8,128)S(1)} fusion(bf16[1024,2048]{1,0:T(8,128)(2,1)} %bitcast.94, bf16[1,2048,1024]{2,1,0:T(8,128)(2,1)} %param.17), kind=kOutput, calls=%fused_computation.16 | convolution fusion | flops 4294967296 | bytes 12582912 | tf_op jit(solution)/shard_map/dot_general | solution.py:92
  205.7 6.5 %multiply_convert_fusion.2 = (bf16[1024,1024]{1,0:T(8,128)(2,1)S(1)}, f32[1024,1024]{1,0:T(8,128)}) fusion(f32[1024,1024]{1,0:T(8,128)S(1)} %fusion.11, bf16[1024,2048]{1,0:T(8,128)(2,1)S(1)} %bitcast.95, bf16[1,2048,1024]{2,1,0:T(8,128)(2,1)S(1)} %copy-done.10), kind=kOutput, calls=%fused_computation.20 | convolution fusion | flops 4301258752 | bytes 18874368 | tf_op jit(solution)/shard_map/dot_general | solution.py:93
  212.2 6.1 %fusion.14 = bf16[16,64,2048]{2,1,0:T(8,128)(2,1)} fusion(bf16[16,64,1024]{2,1,0:T(8,128)(2,1)S(1)} %bitcast.97, bf16[1,1024,2048]{2,1,0:T(8,128)(2,1)S(1)} %copy-done.9), kind=kOutput, calls=%fused_computation.24 | convolution fusion | flops 4297064448 | bytes 10485760 | tf_op jit(solution)/shard_map/dot_general | solution.py:95
  218.6 15.3 %all-gather.14.cloned.1.call-done = bf16[16,64,2048]{2,1,0:T(8,128)(2,1)} async-done(((bf16[4,64,2048]{2,1,0:T(8,128)(2,1)}), bf16[16,64,2048]{2,1,0:T(8,128)(2,1)}) %all-gather.14.cloned.1.call-update) | async-done | bytes 4194320 | tf_op jit(solution)/shard_map/all_gather | solution.py:109
  233.9 7.7 %fusion.3 = f32[1024,1024]{1,0:T(8,128)S(1)} fusion(bf16[1024,2048]{1,0:T(8,128)(2,1)} %bitcast.93, bf16[1,1024,2048]{2,1,0:T(8,128)(2,1)} %param.19), kind=kOutput, calls=%fused_computation.8 | convolution fusion | flops 4294967296 | bytes 12582912 | tf_op jit(solution)/shard_map/dot_general | solution.py:17
  241.7 6.9 %fusion.5 = f32[1024,2048]{1,0:T(8,128)} fusion(bf16[1,2048,1024]{2,1,0:T(8,128)(2,1)S(1)} %copy-done.11, f32[1024,1024]{1,0:T(8,128)S(1)} %fusion.3, f32[1024,1024]{1,0:T(8,128)S(1)} %copy-done.15), kind=kOutput, calls=%fused_computation.10 | convolution fusion | flops 4301258752 | bytes 20971520 | tf_op jit(solution)/shard_map/dot_general | solution.py:17
  248.5 14.3 %add_convert_fusion = bf16[1024,2048]{1,0:T(8,128)(2,1)} fusion(f32[1024,2048]{1,0:T(8,128)} %fusion.5, bf16[1,2048,1024]{2,1,0:T(8,128)(2,1)S(1)} %copy-done.12, f32[1024,1024]{1,0:T(8,128)} %copy-done.14, f32[1024,1024]{1,0:T(8,128)} %copy-done.16, f32[1024,1024]{1,0:T(8,128)} %get-tuple-element.33), kind=kOutput, calls=%fused_computation.5 | convolution fusion | flops 4309647360 | bytes 29360128 | tf_op jit(solution)/shard_map/dot_general | solution.py:17
  262.9 18.0 %reduce-scatter.5.cloned.1.call-done = bf16[4,64,2048]{2,1,0:T(8,128)(2,1)} async-done(((bf16[16,64,2048]{2,1,0:T(8,128)(2,1)}), bf16[4,64,2048]{2,1,0:T(8,128)(2,1)}) %reduce-scatter.5.cloned.1.call-update) | async-done | bytes 1048592 | tf_op jit(solution)/shard_map/reduce_scatter | solution.py:96
  280.9 4.6 all-to-all-start.1
  285.5 42.6 %reduce-scatter.7.cloned.1.call-done = bf16[4,64,2048]{2,1,0:T(8,128)(2,1)} async-done(((bf16[16,64,2048]{2,1,0:T(8,128)(2,1)}), bf16[4,64,2048]{2,1,0:T(8,128)(2,1)}) %reduce-scatter.7.cloned.1.call-update) | async-done | bytes 1048592 | tf_op jit(solution)/shard_map/reduce_scatter | solution.py:120
  328.1 4.6 all-to-all-start.3
  332.7 1.7 gather_fusion
  334.4 23.8 %all-to-all-done.3 = bf16[4,64,2048]{2,1,0:T(8,128)(2,1)S(1)} async-done(((bf16[4,64,2048]{2,1,0:T(8,128)(2,1)}), bf16[4,64,2048]{2,1,0:T(8,128)(2,1)S(1)}, u32[]{:S(2)}, u32[]{:S(2)}) %all-to-all-start.3) | async-done | bytes 1048608 | tf_op jit(solution)/shard_map/all_to_all | solution.py:126
  358.2 0.9 gather_fusion.1
  359.5 2.4 add_convert_fusion.1
  361.9 3.2 convolution_convert_fusion
  365.3 3.9 convolution_convert_fusion.3
  369.2 0.8 copy.52
  370.1 2.5 convolution_convert_fusion.1
  372.6 2.3 copy.47
  374.9 1.5 multiply_reduce_fusion
  376.8 63.3 %reduce-scatter.11.cloned.1.call-done = bf16[256,2048]{1,0:T(8,128)(2,1)} async-done(((bf16[1024,2048]{1,0:T(8,128)(2,1)}), bf16[256,2048]{1,0:T(8,128)(2,1)}) %reduce-scatter.11.cloned.1.call-update) | async-done | bytes 1048592 | tf_op jit(solution)/shard_map/reduce_scatter | solution.py:135
  440.6 1.3 copy.46
  442.0 2.8 pad_maximum_fusion
  444.9 34.5 %all-reduce.3.cloned.1.call-done = bf16[256,2048]{1,0:T(8,128)(2,1)} async-done(((bf16[256,2048]{1,0:T(8,128)(2,1)}), bf16[256,2048]{1,0:T(8,128)(2,1)}) %all-reduce.3.cloned.1.call-update) | async-done | bytes 1048592 | tf_op jit(solution)/shard_map/psum | solution.py:141
  479.8 0.9 copy.48
  480.7 33.3 %reduce-scatter.9.cloned.1.call-done = bf16[128,2048]{1,0:T(8,128)(2,1)} async-done(((bf16[512,2048]{1,0:T(8,128)(2,1)}), bf16[128,2048]{1,0:T(8,128)(2,1)}) %reduce-scatter.9.cloned.1.call-update) | async-done | bytes 524304 | tf_op jit(solution)/shard_map/reduce_scatter | solution.py:165
  514.0 1.9 fusion.41
  515.8 40.6 %all-reduce.5.cloned.1.call-done = bf16[256,2048]{1,0:T(8,128)(2,1)} async-done(((bf16[256,2048]{1,0:T(8,128)(2,1)}), bf16[256,2048]{1,0:T(8,128)(2,1)}) %all-reduce.5.cloned.1.call-update) | async-done | bytes 1048592 | tf_op jit(solution)/shard_map/psum | solution.py:141
  556.4 2.8 convert_element_type.123
  (62 shorter events, 2.6 us)
Async XLA Ops:
  7.2 21.8 %all-gather.8.cloned.1.call-start = ((), (), s32[]{:S(2)}) async-start(), calls=%async_computation.9 | async-start | bytes 1310720 | tf_op jit(solution)/shard_map/all_gather | solution.py:48
  7.9 40.1 %all-gather.6.cloned.1.call-start = ((), (), s32[]{:S(2)}) async-start(), calls=%async_computation.8 | async-start | bytes 1310720 | tf_op jit(solution)/shard_map/all_gather | solution.py:47
  9.8 120.6 %all-gather.10.cloned.1.call-start = ((), (), s32[]{:S(2)}) async-start(), calls=%async_computation.10 | async-start | bytes 5242880 | tf_op jit(solution)/shard_map/all_gather | solution.py:66
  10.5 187.5 %all-gather.12.cloned.1.call-start = ((), (), s32[]{:S(2)}) async-start(), calls=%async_computation.11 | async-start | bytes 5242880 | tf_op jit(solution)/shard_map/all_gather | solution.py:90
  30.5 21.0 %copy-start.6 = (bf16[512,1024]{0,1:T(8,128)(2,1)}, bf16[512,1024]{0,1:T(8,128)(2,1)S(1)}, u32[]{:S(2)}) copy-start(bf16[512,1024]{0,1:T(8,128)(2,1)S(1)} %copy.41) | copy-start | bytes 3145732
  50.1 1.4 copy-start
  51.5 82.0 %copy-start.8 = (f32[2048]{0:T(1024)S(1)}, f32[2048]{0:T(1024)}, u32[]{:S(2)}) copy-start(f32[2048]{0:T(1024)} %param.16) | copy-start | bytes 24580
  164.4 69.5 %all-gather.14.cloned.1.call-start = ((), (), s32[]{:S(2)}) async-start(), calls=%async_computation.13 | async-start | bytes 5242880 | tf_op jit(solution)/shard_map/all_gather | solution.py:109
  195.1 85.8 %reduce-scatter.5.cloned.1.call-start = ((), (), s32[]{:S(2)}) async-start(), calls=%async_computation.12 | async-start | bytes 5242880 | tf_op jit(solution)/shard_map/reduce_scatter | solution.py:96
  198.0 7.7 %copy-start.10 = (bf16[1,2048,1024]{2,1,0:T(8,128)(2,1)S(1)}, bf16[1,2048,1024]{2,1,0:T(8,128)(2,1)}, u32[]{:S(2)}) copy-start(bf16[1,2048,1024]{2,1,0:T(8,128)(2,1)} %param.18) | copy-start | bytes 12582916
  198.0 7.7 %copy-start.13 = (bf16[16,64,2048]{2,1,0:T(8,128)(2,1)S(1)}, bf16[16,64,2048]{2,1,0:T(8,128)(2,1)}, u32[]{:S(2)}) copy-start(bf16[16,64,2048]{2,1,0:T(8,128)(2,1)} %all-gather.12.cloned.1.call-done) | copy-start | bytes 12582916
  205.7 6.6 %copy-start.14 = (f32[1024,1024]{1,0:T(8,128)}, f32[1024,1024]{1,0:T(8,128)S(1)}, u32[]{:S(2)}) copy-start(f32[1024,1024]{1,0:T(8,128)S(1)} %fusion.11) | copy-start | bytes 12582916
  205.7 6.6 %copy-start.9 = (bf16[1,1024,2048]{2,1,0:T(8,128)(2,1)S(1)}, bf16[1,1024,2048]{2,1,0:T(8,128)(2,1)}, u32[]{:S(2)}) copy-start(bf16[1,1024,2048]{2,1,0:T(8,128)(2,1)} %param.19) | copy-start | bytes 12582916
  218.4 109.7 %reduce-scatter.7.cloned.1.call-start = ((), (), s32[]{:S(2)}) async-start(), calls=%async_computation.14 | async-start | bytes 5242880 | tf_op jit(solution)/shard_map/reduce_scatter | solution.py:120
  233.9 7.7 %copy-start.11 = (bf16[1,2048,1024]{2,1,0:T(8,128)(2,1)S(1)}, bf16[1,2048,1024]{2,1,0:T(8,128)(2,1)}, u32[]{:S(2)}) copy-start(bf16[1,2048,1024]{2,1,0:T(8,128)(2,1)} %param.18) | copy-start | bytes 12582916
  233.9 7.7 %copy-start.15 = (f32[1024,1024]{1,0:T(8,128)S(1)}, f32[1024,1024]{1,0:T(8,128)}, u32[]{:S(2)}) copy-start(f32[1024,1024]{1,0:T(8,128)} %copy-done.14) | copy-start | bytes 12582916
  241.7 6.9 %copy-start.16 = (f32[1024,1024]{1,0:T(8,128)}, f32[1024,1024]{1,0:T(8,128)S(1)}, u32[]{:S(2)}) copy-start(f32[1024,1024]{1,0:T(8,128)S(1)} %fusion.3) | copy-start | bytes 12582916
  241.7 6.9 %copy-start.12 = (bf16[1,2048,1024]{2,1,0:T(8,128)(2,1)S(1)}, bf16[1,2048,1024]{2,1,0:T(8,128)(2,1)}, u32[]{:S(2)}) copy-start(bf16[1,2048,1024]{2,1,0:T(8,128)(2,1)} %param.17) | copy-start | bytes 12582916
  280.9 47.2 %all-to-all-start.1 = ((bf16[4,64,2048]{2,1,0:T(8,128)(2,1)}), bf16[4,64,2048]{2,1,0:T(8,128)(2,1)S(1)}, u32[]{:S(2)}, u32[]{:S(2)}) async-start(bf16[4,64,2048]{2,1,0:T(8,128)(2,1)} %reduce-scatter.5.cloned.1.call-done), calls=%async_computation.2 | async-start | bytes 2097152 | tf_op jit(solution)/shard_map/all_to_all | solution.py:102
  328.1 30.1 %all-to-all-start.3 = ((bf16[4,64,2048]{2,1,0:T(8,128)(2,1)}), bf16[4,64,2048]{2,1,0:T(8,128)(2,1)S(1)}, u32[]{:S(2)}, u32[]{:S(2)}) async-start(bf16[4,64,2048]{2,1,0:T(8,128)(2,1)} %reduce-scatter.7.cloned.1.call-done), calls=%async_computation.5 | async-start | bytes 2097152 | tf_op jit(solution)/shard_map/all_to_all | solution.py:126
  332.7 107.5 %reduce-scatter.11.cloned.1.call-start = ((), (), s32[]{:S(2)}) async-start(), calls=%async_computation.16 | async-start | bytes 5242880 | tf_op jit(solution)/shard_map/reduce_scatter | solution.py:135
  359.2 2.7 copy-start.5
  361.9 3.5 copy-start.2
  365.0 5.0 copy-start.1
  365.1 114.3 %all-reduce.3.cloned.1.call-start = ((), (), s32[]{:S(2)}) async-start(), calls=%async_computation.17 | async-start | bytes 2097152 | tf_op jit(solution)/shard_map/psum | solution.py:141
  370.1 4.8 copy-start.7
  376.8 65.2 %copy-start.4 = (bf16[512,1024]{1,0:T(8,128)(2,1)S(1)}, bf16[512,1024]{1,0:T(8,128)(2,1)}, u32[]{:S(2)}) copy-start(bf16[512,1024]{1,0:T(8,128)(2,1)} %copy.47) | copy-start | bytes 3145732
  440.2 73.8 %reduce-scatter.9.cloned.1.call-start = ((), (), s32[]{:S(2)}) async-start(), calls=%async_computation.15 | async-start | bytes 2621440 | tf_op jit(solution)/shard_map/reduce_scatter | solution.py:165
  442.0 37.4 %copy-start.3 = (bf16[512,1024]{0,1:T(8,128)(2,1)S(1)}, bf16[512,1024]{0,1:T(8,128)(2,1)}, u32[]{:S(2)}) copy-start(bf16[512,1024]{0,1:T(8,128)(2,1)} %all-gather.6.cloned.1.call-done) | copy-start | bytes 3145732
  444.8 111.6 %all-reduce.5.cloned.1.call-start = ((), (), s32[]{:S(2)}) async-start(), calls=%async_computation.18 | async-start | bytes 2097152 | tf_op jit(solution)/shard_map/psum | solution.py:141
Sparse Core Ops, SparseCore 0:
  9.5 19.4 all-gather.7
  31.1 16.8 all-gather.5
  49.5 80.7 all-gather.9
  164.5 33.4 all-gather.11
  199.4 34.4 all-gather.13
  236.3 44.5 reduce-scatter.4
  283.4 44.5 reduce-scatter.6
  365.2 74.9 reduce-scatter.10
  442.5 36.8 all-reduce.2
  482.3 31.6 reduce-scatter.8
  516.3 40.0 all-reduce.4
